TPU v7x, 32 devices: a whole 2x2x4 slice. The times are simulated.
32 devices in a mesh: dp: 4 (over x, core), seq: 8 (over z, y).
Axes of the slice: x: 2, y: 2, z: 4, core: 2. Of those that a mesh axis runs over, the one named last changes fastest.
Arguments:
- xbc_in: bfloat16 [4, 2048, 2816], P('dp', 'seq'), may hold values from -4 to 4
- conv_weight: float32 [4, 2816], replicated, may hold values from -3 to 3
- conv_bias: float32 [2816], replicated, may hold values from -3 to 3
- step_sizes: float32 [4, 40, 2048], P('dp', None, 'seq'), may hold values from 0 to 1, as said below
- decay_rates: float32 [40], replicated, may hold values from 0.7 to 1.4
- skip_gain: float32 [40], replicated, may hold values from 0.5 to 1.5
- grad_out: bfloat16 [4, 2048, 2560], P('dp', 'seq'), may hold values from -0.75 to 0.75
Outputs:
- grad_xbc: bfloat16 [4, 2048, 2816], P('dp', 'seq')
- grad_steps: float32 [4, 40, 2048], P('dp', None, 'seq')
- grad_conv_weight: float32 [4, 2816], replicated
- grad_conv_bias: float32 [2816], replicated
- grad_rates: float32 [40], replicated
- grad_skip: float32 [40], replicated
Inputs may be any that keep to these rules, and one draw needn't show every extreme that they name: `step_sizes`: positive step sizes.
All inputs are finite; a program needn't handle non-finite values.
Results may differ from a plain program's by a relative error of at most 0.0056.
Values may be sent and summed in bfloat16 or wider, within the bound.
A program may use at most 192 MiB of HBM per device.

v0:
```python
import jax
import jax.numpy as jnp
from jax import lax
from jax.sharding import PartitionSpec as P

HEADS = 40
HEAD_DIM = 64
STATE = 128
GROUP = 256
KCONV = 4


def shifted(array, axis, by):
    length = lax.axis_size(axis)
    pairs = [(i, i + by) for i in range(length) if 0 <= i + by < length]
    return lax.ppermute(array, axis, pairs)


def carried_in(array, axis, combine, identity, reverse):
    length, place = (lax.axis_size(axis), lax.axis_index(axis))
    everything = jax.tree.map(lambda part: lax.all_gather(part, axis), array)
    start = jax.tree.map(
        lambda part, zero: jnp.broadcast_to(jnp.asarray(zero, part.dtype), part.shape),
        array,
        identity,
    )

    def lap(k, before):
        at = length - 1 - k if reverse else k
        reached = at > place if reverse else at < place
        new = combine(before, jax.tree.map(lambda part: part[at], everything))
        return jax.tree.map(lambda a, b: jnp.where(reached, a, b), new, before)

    return lax.fori_loop(0, length, lap, start)


def silu_pair(pre_act):
    sigmoid_v = jax.nn.sigmoid(pre_act)
    return (pre_act * sigmoid_v, sigmoid_v * (1.0 + pre_act * (1.0 - sigmoid_v)))


def block_locals(z_block, dy_block, cum_log):
    x_width = HEADS * HEAD_DIM
    b_proj = z_block[:, x_width : x_width + STATE]
    c_proj = z_block[:, x_width + STATE :]
    log_end = cum_log[:, -1:]
    tail_wide = jnp.repeat(jnp.exp(log_end - cum_log).T, HEAD_DIM, axis=1)
    head_wide = jnp.repeat(jnp.exp(cum_log).T, HEAD_DIM, axis=1)
    x_weighted = (z_block[:, :x_width].astype(jnp.float32) * tail_wide).astype(jnp.bfloat16)
    dy_weighted = (dy_block.astype(jnp.float32) * head_wide).astype(jnp.bfloat16)
    contract_rows = (((0,), (0,)), ((), ()))
    s_local = lax.dot_general(x_weighted, b_proj, contract_rows, preferred_element_type=jnp.float32)
    u_local = lax.dot_general(
        dy_weighted, c_proj, contract_rows, preferred_element_type=jnp.float32
    )
    s_local = s_local.reshape(HEADS, HEAD_DIM, STATE)
    u_local = u_local.reshape(HEADS, HEAD_DIM, STATE)
    return (s_local, u_local, x_weighted, dy_weighted)


def block_grads(
    z_block, dy_block, cum_log, x_weighted, dy_weighted, start_state, end_adjoint, skip_gain
):
    x_width = HEADS * HEAD_DIM
    x_flat = z_block[:, :x_width]
    b_proj = z_block[:, x_width : x_width + STATE]
    c_proj = z_block[:, x_width + STATE :]
    log_end = cum_log[:, -1:]
    contract_last = (((1,), (1,)), ((), ()))
    gram_bc = lax.dot_general(b_proj, c_proj, contract_last, preferred_element_type=jnp.float32)
    row_index = lax.broadcasted_iota(jnp.int32, (GROUP, GROUP), 0)
    col_index = lax.broadcasted_iota(jnp.int32, (GROUP, GROUP), 1)
    causal = (row_index >= col_index)[None]
    upper = (row_index <= col_index)[None]
    log_gap = cum_log[:, :, None] - cum_log[:, None, :]
    decay_lower = jnp.where(causal, jnp.exp(jnp.where(causal, log_gap, 0.0)), 0.0)
    rise_gap = cum_log[:, None, :] - cum_log[:, :, None]
    decay_upper = jnp.where(upper, jnp.exp(jnp.where(upper, rise_gap, 0.0)), 0.0)
    x_heads = x_flat.reshape(GROUP, HEADS, HEAD_DIM)
    dy_heads = dy_block.reshape(GROUP, HEADS, HEAD_DIM)
    inner_dx = jnp.einsum("thp,shp->hts", dy_heads, x_heads, preferred_element_type=jnp.float32)
    weights = decay_lower * inner_dx
    k_matrix = (decay_upper * gram_bc[None]).astype(jnp.bfloat16)
    m_terms = weights * gram_bc.T[None]
    w_summed = jnp.sum(weights, axis=0).astype(jnp.bfloat16)
    states_low = start_state.astype(jnp.bfloat16).reshape(x_width, STATE)
    adjoint_low = end_adjoint.astype(jnp.bfloat16).reshape(x_width, STATE)
    b_adjoint = lax.dot_general(
        b_proj, adjoint_low, contract_last, preferred_element_type=jnp.float32
    )
    tail_wide = jnp.repeat(jnp.exp(log_end - cum_log).T, HEAD_DIM, axis=1)
    intra_dx = jnp.einsum("hts,shp->thp", k_matrix, dy_heads, preferred_element_type=jnp.float32)
    dx_state = intra_dx.reshape(GROUP, x_width) + tail_wide * b_adjoint
    contract_rows = (((0,), (0,)), ((), ()))
    grad_bproj = lax.dot_general(
        w_summed, c_proj, contract_rows, preferred_element_type=jnp.float32
    )
    grad_bproj = grad_bproj + jnp.dot(x_weighted, adjoint_low, preferred_element_type=jnp.float32)
    grad_cproj = jnp.dot(w_summed, b_proj, preferred_element_type=jnp.float32)
    grad_cproj = grad_cproj + jnp.dot(dy_weighted, states_low, preferred_element_type=jnp.float32)
    c_state = lax.dot_general(c_proj, states_low, contract_last, preferred_element_type=jnp.float32)
    x_float = x_flat.astype(jnp.float32)
    dy_float = dy_block.astype(jnp.float32)
    q_terms = jnp.sum((c_state * dy_float).reshape(GROUP, HEADS, HEAD_DIM), axis=2).T
    r_terms = jnp.sum((b_adjoint * x_float).reshape(GROUP, HEADS, HEAD_DIM), axis=2).T
    col_sums = jnp.sum(m_terms, axis=1)
    row_sums = jnp.sum(m_terms, axis=2)
    term_one = jnp.cumsum(col_sums - row_sums, axis=1) + row_sums
    term_two = jnp.flip(jnp.cumsum(jnp.flip(jnp.exp(cum_log) * q_terms, 1), axis=1), 1)
    term_three = jnp.cumsum(jnp.exp(log_end - cum_log) * r_terms, axis=1)
    term_four = jnp.exp(log_end) * jnp.sum(end_adjoint * start_state, axis=(1, 2))[:, None]
    own_terms = jnp.sum((x_float * dx_state).reshape(GROUP, HEADS, HEAD_DIM), axis=2).T
    grad_log = term_one + term_two + term_three + term_four - own_terms
    dx_full = dx_state + jnp.repeat(skip_gain, HEAD_DIM)[None, :] * dy_float
    grad_z = jnp.concatenate([dx_full, grad_bproj, grad_cproj], axis=1)
    return (grad_z, grad_log)


def compose(earlier, later):
    return (earlier[0] * later[0], later[0][:, :, None, None] * earlier[1] + later[1])


def shards(xbc_in, conv_weight, conv_bias, step_sizes, decay_rates, skip_gain, grad_out):
    seq_count, tokens, channels = xbc_in.shape
    rim_len = KCONV - 1
    x_width = HEADS * HEAD_DIM
    block_count = tokens // GROUP
    before = shifted(xbc_in[:, tokens - rim_len :, :], "seq", 1)
    padded_in = jnp.concatenate([before, xbc_in], axis=1)
    pre_act = jnp.zeros((seq_count, tokens, channels), jnp.float32) + conv_bias[None, None, :]
    for tap_index in range(KCONV):
        pre_act = pre_act + conv_weight[tap_index][None, None, :] * padded_in[
            :, tap_index : tap_index + tokens
        ].astype(jnp.float32)
    activated, derivative = silu_pair(pre_act)
    z_seq = activated.astype(jnp.bfloat16)
    skip_terms = (z_seq[:, :, :x_width].astype(jnp.float32) * grad_out.astype(jnp.float32)).reshape(
        seq_count, tokens, HEADS, HEAD_DIM
    )
    local_skip = jnp.sum(skip_terms, axis=(0, 1, 3))
    log_steps = -(step_sizes * decay_rates[None, :, None])
    cum_log = jnp.cumsum(log_steps.reshape(seq_count, HEADS, block_count, GROUP), axis=3)
    locals_fn = jax.vmap(block_locals)
    grads_fn = jax.vmap(block_grads, in_axes=(0, 0, 0, 0, 0, 0, 0, None))
    block_index = 0
    z_parts = [z_seq]
    dy_parts = [grad_out]
    log_parts = [cum_log[:, :, block_index]]
    local_items = [locals_fn(z_parts[block_index], dy_parts[block_index], log_parts[block_index])]
    decay_ends = [jnp.exp(log_parts[block_index][:, :, -1])]
    dev_decay = jnp.ones((seq_count, HEADS), jnp.float32)
    dev_state = jnp.zeros((seq_count, HEADS, HEAD_DIM, STATE), jnp.float32)
    dev_adjoint = jnp.zeros((seq_count, HEADS, HEAD_DIM, STATE), jnp.float32)
    block_index = 0
    dev_state = decay_ends[block_index][:, :, None, None] * dev_state + local_items[block_index][0]
    dev_decay = dev_decay * decay_ends[block_index]
    for block_index in reversed(range(block_count)):
        dev_adjoint = (
            decay_ends[block_index][:, :, None, None] * dev_adjoint + local_items[block_index][1]
        )
    identity_pair = (jnp.ones_like(dev_decay), jnp.zeros_like(dev_state))
    enter_pair = carried_in((dev_decay, dev_state), "seq", compose, identity_pair, False)
    leave_pair = carried_in((dev_decay, dev_adjoint), "seq", compose, identity_pair, True)
    entering = enter_pair[1]
    leaving = leave_pair[1]
    block_index = 0
    block_starts = [entering]
    adjoint_run = leaving
    block_ends = [adjoint_run] * block_count
    for block_index in reversed(range(block_count)):
        block_ends[block_index] = adjoint_run
        adjoint_run = (
            decay_ends[block_index][:, :, None, None] * adjoint_run + local_items[block_index][1]
        )
    block_index = 0
    grad_piece, log_piece = grads_fn(
        z_parts[block_index],
        dy_parts[block_index],
        log_parts[block_index],
        local_items[block_index][2],
        local_items[block_index][3],
        block_starts[block_index],
        block_ends[block_index],
        skip_gain,
    )
    grad_pre = grad_piece * derivative
    tail_zeros = jnp.zeros((seq_count, rim_len, channels), jnp.float32)
    padded_grad = jnp.concatenate([grad_pre, tail_zeros], axis=1)
    front_rows = jnp.concatenate([tail_zeros, grad_pre[:, :rim_len]], axis=1)
    grad_in = jnp.zeros((seq_count, tokens, channels), jnp.float32)
    partial_rows = jnp.zeros((seq_count, rim_len, channels), jnp.float32)
    for tap_index in range(KCONV):
        tap_start = rim_len - tap_index
        grad_in = (
            grad_in
            + conv_weight[tap_index][None, None, :] * padded_grad[:, tap_start : tap_start + tokens]
        )
        partial_rows = (
            partial_rows
            + conv_weight[tap_index][None, None, :] * front_rows[:, tap_start : tap_start + rim_len]
        )
    incoming = shifted(partial_rows, "seq", -1)
    grad_in = jnp.concatenate(
        [grad_in[:, : tokens - rim_len], grad_in[:, tokens - rim_len :] + incoming], axis=1
    )
    grad_taps = []
    for tap_index in range(KCONV):
        grad_taps.append(
            jnp.sum(
                grad_pre * padded_in[:, tap_index : tap_index + tokens].astype(jnp.float32),
                axis=(0, 1),
            )
        )
    local_weight = jnp.stack(grad_taps)
    local_bias = jnp.sum(grad_pre, axis=(0, 1))
    local_rates = -jnp.sum(step_sizes * log_piece, axis=(0, 2))
    grad_steps = -decay_rates[None, :, None] * log_piece
    grad_weight, grad_bias, grad_rates, grad_skip = lax.psum(
        (local_weight, local_bias, local_rates, local_skip), ("dp", "seq")
    )
    return (grad_in.astype(jnp.bfloat16), grad_steps, grad_weight, grad_bias, grad_rates, grad_skip)


def solution(mesh):
    return jax.shard_map(
        shards,
        mesh=mesh,
        in_specs=(
            P("dp", "seq", None),
            P(),
            P(),
            P("dp", None, "seq"),
            P(),
            P(),
            P("dp", "seq", None),
        ),
        out_specs=(P("dp", "seq", None), P("dp", None, "seq"), P(), P(), P(), P()),
        check_vma=False,
    )
```

profile of v0, /device:TPU:0, one launch (start us, length us, event | category | flops | bytes accessed | tf_op | source)
XLA Modules:
  0.0 455.2 jit_solution(9442393035926646633)
XLA Ops:
  8.0 4.9 %collective-permute-start = (bf16[1,3,2816]{2,1,0:T(4,128)(2,1)S(1)}, bf16[1,3,2816]{2,1,0:T(4,128)(2,1)S(1)}, u32[]{:S(2)}, u32[]{:S(2)}) collective-permute-start(bf16[1,3,2816]{2,1,0:T(4,128)(2,1)S(1)} %slice.105), channel_id=1, source_target_pairs={{0,1},{1,2},{2,3},{3,4},{4,5},{5,6},{6,7},{8,9},{9,10},{10,11},{11... | collective-permute-start | bytes 50696 | tf_op jit(solution)/shard_map/ppermute | solution.py:16
  14.9 1.7 broadcast_in_dim.65
  16.6 3.3 copy.237
  20.0 2.0 fusion.62
  22.7 1.4 copy.238
  24.2 4.4 multiply_convert_fusion.2
  28.6 1.1 copy-done.2
  29.7 1.7 convolution_add_fusion.1
  31.5 1.4 copy.231
  34.4 1.7 broadcast_in_dim.63
  36.1 3.2 copy.244
  39.3 3.6 copy.241
  42.9 19.1 %all-gather = f32[8,40,1]{1,2,0:T(1,128)S(1)} all-gather(f32[1,40,1]{1,2,0:T(1,128)S(1)} %get-tuple-element.428), channel_id=2, replica_groups=mesh['dp'=4,'seq'=8] {'seq'}, dimensions={0}, use_global_device_ids=true | all-gather | bytes 1440 | tf_op jit(solution)/shard_map/all_gather | solution.py:21
  63.3 5.4 %fusion.2 = f32[40,256,64]{1,2,0:T(8,128)} fusion(bf16[256,40,64]{0,2,1:T(8,128)(2,1)} %bitcast.195, f32[256,256]{0,1:T(8,128)S(1)} %copy.230, f32[40,256]{1,0:T(8,128)S(1)} %bitcast_add_fusion.3, pred[256,256]{0,1:T(8,128)(4,1)S(1)} %iota_compare_fusion.1), kind=kOutput, calls=%fused_computation.10 | convolution fusion | flops 348651520 | bytes 4300800 | tf_op jit(solution)/shard_map/vmap(hts,shp->thp)/dot_general | solution.py:92
  68.7 3.3 copy.242
  72.0 110.4 %all-gather.6.cloned.1.call-done = f32[320,64,128]{2,1,0:T(8,128)} async-done(((f32[40,64,128]{2,1,0:T(8,128)}), f32[320,64,128]{2,1,0:T(8,128)}) %all-gather.6.cloned.1.call-update) | async-done | bytes 10485776 | tf_op jit(solution)/shard_map/all_gather | solution.py:21
  182.3 13.3 %while.30 = (s32[]{:T(128)}, f32[1,40,64,128]{3,2,1,0:T(8,128)S(1)}, s32[]{:T(128)}, f32[8,1,40]{2,1,0:T(1,128)S(1)}, f32[8,1,40,64,128]{4,3,2,1,0:T(8,128)}, /*index=5*/s32[]{:T(128)}, s32[]{:T(128)}, s32[]{:T(128)}, s32[]{:T(128)}) while((s32[]{:T(128)}, f32[1,40,64,128]{3,2,1,0:T(8,128)S(1)}, s32[]{:T(128)}, ...), condition=%wide.region_3.4_spmd.clone, body=%wide.region_2.3_spmd.clone.sunk | while | flops 1310728 | bytes 3932815 | solution.py:34
  182.3 1.6 fusion.80
  184.0 1.6 fusion.80
  185.7 1.6 fusion.80
  187.4 1.6 fusion.80
  189.0 1.6 fusion.80
  190.7 1.6 fusion.80
  192.4 1.6 fusion.80
  194.0 1.6 fusion.80
  195.8 8.9 %convert_multiply_fusion.1 = (f32[1,256,2560]{2,1,0:T(8,128)}, f32[1,256,2560]{2,1,0:T(8,128)}, f32[1,256,2560]{2,1,0:T(8,128)}, f32[2560]{0:T(1024)}, bf16[2560,256]{0,1:T(8,128)(2,1)}) fusion(f32[256,2560]{1,0:T(8,128)} %copy.242, f32[256,2560]{1,0:T(8,128)} %copy.241, bf16[1,256,2816]{2,1,0:T(8,128)(2,1)} %copy-done.2, ...), kind=kOutput, calls=%fused_computation.17 | convolution fusion | flops 175633920 | bytes 20402176 | tf_op jit(solution)/shard_map/vmap()/dot_general | solution.py:88
  204.8 1.6 copy.247
  206.4 2.4 convolution_add_fusion
  210.0 2.5 slice.138
  212.4 2.5 copy.243
  214.9 7.5 %multiply_reduce_fusion.1 = (f32[40,256]{1,0:T(8,128)S(1)}, f32[40,256]{1,0:T(8,128)S(1)}, bf16[256,256]{0,1:T(8,128)(2,1)S(1)}) fusion(f32[256,256]{0,1:T(8,128)} %bitcast.198, f32[40,256]{1,0:T(8,128)} %copy-done.27, pred[256,256]{0,1:T(8,128)(4,1)} %iota_compare_fusion, bf16[256,40,64]{0,2,1:T(8,128)(2,1)} %bitcast.197, bf16[256,40,64]{0,2,1:T(8,128)(2,1)} %bitcast.196), kind=kOutput, calls=%fused_computation.9 | convolution fusion | flops 356429824 | bytes 3203072 | tf_op jit(solution)/shard_map/vmap(thp,shp->hts)/dot_general | solution.py:81
  223.7 1.4 sub.92
  225.1 1.4 copy.252
  226.5 1.9 reduce-window.30
  228.4 1.4 copy.253
  229.8 1.5 slice_reduce_fusion.2
  232.6 1.4 copy.254
  234.0 3.3 copy.265
  237.3 2.6 reduce_sum.150
  239.9 1.4 reduce_sum.159
  242.1 3.3 copy.260
  245.4 2.6 reduce_sum.147
  248.0 1.5 copy.261
  249.6 2.6 fusion.24
  253.2 104.4 %all-gather.8.cloned.1.call-done = f32[320,64,128]{2,1,0:T(8,128)} async-done(((f32[40,64,128]{2,1,0:T(8,128)}), f32[320,64,128]{2,1,0:T(8,128)}) %all-gather.8.cloned.1.call-update) | async-done | bytes 10485776 | tf_op jit(solution)/shard_map/all_gather | solution.py:21
  357.6 18.2 %while.31 = (s32[]{:T(128)}, f32[1,40,64,128]{3,2,1,0:T(8,128)S(1)}, s32[]{:T(128)}, f32[8,1,40]{2,1,0:T(1,128)}, f32[8,1,40,64,128]{4,3,2,1,0:T(8,128)}, /*index=5*/s32[]{:T(128)}, s32[]{:T(128)}) while((s32[]{:T(128)}, f32[1,40,64,128]{3,2,1,0:T(8,128)S(1)}, s32[]{:T(128)}, f32[8,1,40]{2,1,0:T(1,128)}, ...), condition=%wide.region_6.7_spmd.clone, body=%wide.region_5.6_spmd.clone.sunk | while | flops 1310724 | bytes 3932753 | solution.py:34
  358.2 1.6 fusion.81
  360.5 1.6 fusion.81
  362.8 1.6 fusion.81
  365.0 1.6 fusion.81
  367.3 1.6 fusion.81
  369.6 1.6 fusion.81
  371.9 1.6 fusion.81
  374.2 1.6 fusion.81
  377.2 2.6 fusion.26
  380.9 4.7 %fusion.13 = (f32[2816]{0:T(1024)S(1)}, f32[2816]{0:T(1024)S(1)}, f32[2816]{0:T(1024)S(1)}, f32[2816]{0:T(1024)S(1)}, f32[2816]{0:T(1024)S(1)}, /*index=5*/f32[1,256,2816]{2,1,0:T(8,128)S(1)}) fusion(bf16[1,256,2816]{2,1,0:T(8,128)(2,1)S(1)} %copy-done.4, bf16[1,3,2816]{2,1,0:T(4,128)(2,1)S(1)} %copy-done.20, f32[2816]{0:T(1024)S(1)} %copy-done.13, ...), kind=kLoop, calls=%fused_computation.37 | loop fusion | flops 34588928 | bytes 7338496 | tf_op jit(solution)/shard_map/reduce_sum | solution.py:209
  385.6 2.8 multiply_add_fusion
  388.4 2.9 convert_multiply_fusion.4
  391.3 3.2 copy.255
  394.5 2.1 reduce_sum.145
  398.8 1.3 collective-permute-start.1
  402.0 2.0 slice.261
  404.6 41.7 %all-reduce.2 = (f32[4,2816]{1,0:T(4,128)}, f32[2816]{0:T(1024)}, f32[40]{0:T(128)}, f32[40]{0:T(128)}) all-reduce(f32[4,2816]{1,0:T(4,128)S(1)} %pad_maximum_fusion.2, f32[2816]{0:T(1024)S(1)} %get-tuple-element.383, f32[40]{0:T(128)S(1)} %neg.16, f32[40]{0:T(128)S(1)} %reduce_sum.160), channel_id=1, replica_groups=mesh['dp'=4,'seq'=8] {'dp','seq'}, use_global_device_ids=true, to_apply=%region_23.24 | all-reduce | flops 14160 | bytes 113280 | tf_op jit(solution)/shard_map/psum | solution.py:218
  447.2 1.2 pad_maximum_fusion.1
  (162 shorter events, 24.7 us)
Async XLA Ops:
  7.2 175.2 %all-gather.6.cloned.1.call-start = ((), (), s32[]{:S(2)}) async-start(), calls=%async_computation | async-start | bytes 11796480 | tf_op jit(solution)/shard_map/all_gather | solution.py:21
  8.0 16.1 %collective-permute-start = (bf16[1,3,2816]{2,1,0:T(4,128)(2,1)S(1)}, bf16[1,3,2816]{2,1,0:T(4,128)(2,1)S(1)}, u32[]{:S(2)}, u32[]{:S(2)}) collective-permute-start(bf16[1,3,2816]{2,1,0:T(4,128)(2,1)S(1)} %slice.105), channel_id=1, source_target_pairs={{0,1},{1,2},{2,3},{3,4},{4,5},{5,6},{6,7},{8,9},{9,10},{10,11},{11... | collective-permute-start | bytes 50696 | tf_op jit(solution)/shard_map/ppermute | solution.py:16
  16.6 3.4 copy-start
  20.0 2.0 copy-start.26
  22.0 2.1 copy-start.22
  22.7 5.9 %copy-start.8 = (f32[2816]{0:T(1024)}, f32[2816]{0:T(1024)S(1)}, u32[]{:S(2)}) copy-start(f32[2816]{0:T(1024)S(1)} %get-tuple-element.386) | copy-start | bytes 33796
  22.7 5.9 %copy-start.10 = (f32[2816]{0:T(1024)}, f32[2816]{0:T(1024)S(1)}, u32[]{:S(2)}) copy-start(f32[2816]{0:T(1024)S(1)} %get-tuple-element.388) | copy-start | bytes 33796
  22.7 5.9 %copy-start.12 = (f32[2816]{0:T(1024)}, f32[2816]{0:T(1024)S(1)}, u32[]{:S(2)}) copy-start(f32[2816]{0:T(1024)S(1)} %get-tuple-element.387) | copy-start | bytes 33796
  24.1 5.6 %copy-start.5 = (bf16[2560,256]{1,0:T(8,128)(2,1)S(1)}, bf16[2560,256]{1,0:T(8,128)(2,1)}, u32[]{:S(2)}) copy-start(bf16[2560,256]{1,0:T(8,128)(2,1)} %copy.238) | copy-start | bytes 3932164
  24.2 7.2 %copy-start.19 = (bf16[1,3,2816]{2,1,0:T(4,128)(2,1)}, bf16[1,3,2816]{2,1,0:T(4,128)(2,1)S(1)}, u32[]{:S(2)}) copy-start(bf16[1,3,2816]{2,1,0:T(4,128)(2,1)S(1)} %collective-permute-done) | copy-start | bytes 50692
  28.6 1.1 copy-start.2
  31.4 1.5 copy-start.33
  31.4 326.2 %all-gather.8.cloned.1.call-start = ((), (), s32[]{:S(2)}) async-start(), calls=%async_computation.1 | async-start | bytes 11796480 | tf_op jit(solution)/shard_map/all_gather | solution.py:21
  33.8 0.5 copy-start.29
  62.0 6.7 %copy-start.27 = (f32[40,256]{1,0:T(8,128)}, f32[40,256]{1,0:T(8,128)S(1)}, u32[]{:S(2)}) copy-start(f32[40,256]{1,0:T(8,128)S(1)} %bitcast_add_fusion.3) | copy-start | bytes 122884
  63.1 5.6 %copy-start.6 = (f32[256,256]{1,0:T(8,128)}, f32[256,256]{1,0:T(8,128)S(1)}, u32[]{:S(2)}) copy-start(f32[256,256]{1,0:T(8,128)S(1)} %fusion.35) | copy-start | bytes 786436
  182.3 13.4 %copy-start.24 = (f32[2560]{0:T(1024)S(1)}, f32[2560]{0:T(1024)}, u32[]{:S(2)}) copy-start(f32[2560]{0:T(1024)} %mul.301) | copy-start | bytes 30724
  195.7 9.1 %copy-start.28 = (f32[8,1,40]{2,1,0:T(1,128)}, f32[8,1,40]{2,1,0:T(1,128)S(1)}, u32[]{:S(2)}) copy-start(f32[8,1,40]{2,1,0:T(1,128)S(1)} %get-tuple-element.551) | copy-start | bytes 3844
  206.3 2.4 copy-start.31
  222.5 0.6 copy-start.16
  375.8 1.3 copy-start.1
  376.3 4.6 %copy-start.3 = (f32[1,256,2560]{2,1,0:T(8,128)S(1)}, f32[1,256,2560]{2,1,0:T(8,128)}, u32[]{:S(2)}) copy-start(f32[1,256,2560]{2,1,0:T(8,128)} %get-tuple-element.419) | copy-start | bytes 7864324
  376.3 4.6 %copy-start.4 = (bf16[1,256,2816]{2,1,0:T(8,128)(2,1)S(1)}, bf16[1,256,2816]{2,1,0:T(8,128)(2,1)}, u32[]{:S(2)}) copy-start(bf16[1,256,2816]{2,1,0:T(8,128)(2,1)} %param.11) | copy-start | bytes 4325380
  376.3 4.6 %copy-start.9 = (f32[2816]{0:T(1024)S(1)}, f32[2816]{0:T(1024)}, u32[]{:S(2)}) copy-start(f32[2816]{0:T(1024)} %copy-done.8) | copy-start | bytes 33796
  376.3 4.6 %copy-start.11 = (f32[2816]{0:T(1024)S(1)}, f32[2816]{0:T(1024)}, u32[]{:S(2)}) copy-start(f32[2816]{0:T(1024)} %copy-done.10) | copy-start | bytes 33796
  376.3 4.6 %copy-start.13 = (f32[2816]{0:T(1024)S(1)}, f32[2816]{0:T(1024)}, u32[]{:S(2)}) copy-start(f32[2816]{0:T(1024)} %copy-done.12) | copy-start | bytes 33796
  376.3 4.6 %copy-start.20 = (bf16[1,3,2816]{2,1,0:T(4,128)(2,1)S(1)}, bf16[1,3,2816]{2,1,0:T(4,128)(2,1)}, u32[]{:S(2)}) copy-start(bf16[1,3,2816]{2,1,0:T(4,128)(2,1)} %copy-done.19) | copy-start | bytes 50692
  376.3 4.6 %copy-start.23 = (f32[2816]{0:T(1024)S(1)}, f32[2816]{0:T(1024)}, u32[]{:S(2)}) copy-start(f32[2816]{0:T(1024)} %param.13) | copy-start | bytes 33796
  394.5 2.3 copy-start.7
  394.5 2.3 copy-start.30
  394.5 4.3 copy-start.25
  394.5 6.5 %copy-start.21 = (f32[40,2]{1,0:T(8,128)S(1)}, f32[40,2]{1,0:T(8,128)}, u32[]{:S(2)}) copy-start(f32[40,2]{1,0:T(8,128)} %copy.254) | copy-start | bytes 964
  394.5 6.7 %copy-start.14 = (f32[1,40,256]{2,1,0:T(8,128)S(1)}, f32[1,40,256]{2,1,0:T(8,128)}, u32[]{:S(2)}) copy-start(f32[1,40,256]{2,1,0:T(8,128)} %param.14) | copy-start | bytes 122884
  394.5 6.7 %copy-start.15 = (f32[1,40,2,128]{3,2,0,1:T(2,128)S(1)}, f32[1,40,2,128]{3,2,0,1:T(2,128)}, u32[]{:S(2)}) copy-start(f32[1,40,2,128]{3,2,0,1:T(2,128)} %copy.253) | copy-start | bytes 122884
  394.5 6.7 %copy-start.17 = (f32[40,256]{1,0:T(8,128)S(1)}, f32[40,256]{1,0:T(8,128)}, u32[]{:S(2)}) copy-start(f32[40,256]{1,0:T(8,128)} %copy-done.16) | copy-start | bytes 122884
  394.5 6.7 %copy-start.18 = (f32[256,40]{0,1:T(8,128)S(1)}, f32[256,40]{0,1:T(8,128)}, u32[]{:S(2)}) copy-start(f32[256,40]{0,1:T(8,128)} %reduce_sum.150) | copy-start | bytes 122884
  394.5 7.3 %copy-start.32 = (f32[40]{0:T(128)S(1)}, f32[40]{0:T(128)}, u32[]{:S(2)}) copy-start(f32[40]{0:T(128)} %neg.15) | copy-start | bytes 484
  398.8 47.4 %collective-permute-start.1 = (f32[1,3,2816]{2,1,0:T(4,128)S(1)}, f32[1,3,2816]{2,1,0:T(4,128)S(1)}, u32[]{:S(2)}, u32[]{:S(2)}) collective-permute-start(f32[1,3,2816]{2,1,0:T(4,128)S(1)} %fusion.46), channel_id=1, source_target_pairs={{1,0},{2,1},{3,2},{4,3},{5,4},{6,5},{7,6},{9,8},{10,9},{11,10},{12... | collective-permute-start | bytes 101384 | tf_op jit(solution)/shard_map/ppermute | solution.py:16
Sparse Core Ops, SparseCore 0:
  31.6 150.7 all-gather.5
  208.9 148.6 all-gather.7
where the time goes:
time: 457 us; the launch traced here: 455 us
  waiting for transfers between devices  215 us (47%)
  local copies, waits for them, and re-layouts  61.2 us (13%)
  blocking collectives  60.8 us (13%)
  other arithmetic  59.6 us (13%)
  matrix products  37.2 us (8%)
  between operations  14.8 us (3%)
  starting transfers between devices  6.27 us (1%)
    all_gather x2, waiting for transfers between devices, carried_in(): everything = jax.tree.map(lambda part: lax.all_gather(part, axis), array)  215 us
    psum x1, blocking collectives, shards(): lax.psum((local_weight, local_bias, local_rates, local_skip), ('dp', 'seq'))  41.7 us
    select_n x16, other arithmetic, lap(): return jax.tree.map(lambda a, b: jnp.where(reached, a, b), new, before)  25.9 us
    all_gather x1, blocking collectives, carried_in(): everything = jax.tree.map(lambda part: lax.all_gather(part, axis), array)  19.1 us
  transfers between devices with their start and end apart: 4, of which 2 were waited for; matrix products, arithmetic and copies ran while one was open for 18% of the time, Pallas kernels for 0%

commit v1 on v0

--- a/solution.py
+++ b/solution.py
@@ -216,7 +216,7 @@
     local_rates = -jnp.sum(step_sizes * log_piece, axis=(0, 2))
     grad_steps = -decay_rates[None, :, None] * log_piece
     grad_weight, grad_bias, grad_rates, grad_skip = lax.psum(
-        (local_weight, local_bias, local_rates, local_skip), ("dp", "seq")
+        lax.psum((local_weight, local_bias, local_rates, local_skip), "seq"), "dp"
     )
     return (grad_in.astype(jnp.bfloat16), grad_steps, grad_weight, grad_bias, grad_rates, grad_skip)
 

time: 457 us -> 464 us (1.015)
  blocking collectives: 60.8 us -> 67.3 us
    psum x1 -> x2, blocking collectives: 41.7 us -> 48.1 us  [the longest x1 36.9 us: shards(): lax.psum((local_weight, local_bias, local_rates, local_skip), 'seq')]
  transfers between devices with their start and end apart: 4 -> 4, of which waited for: 2 -> 2; matrix products, arithmetic and copies ran while one was open for 18% -> 17% of each run, Pallas kernels for 0% -> 0%
where the time goes in v1:
time: 464 us; the launch traced here: 462 us
  waiting for transfers between devices  215 us (46%)
  blocking collectives  67.3 us (15%)
  local copies, waits for them, and re-layouts  61.2 us (13%)
  other arithmetic  59.5 us (13%)
  matrix products  37.2 us (8%)
  between operations  14.8 us (3%)
  starting transfers between devices  6.27 us (1%)
    all_gather x2, waiting for transfers between devices, carried_in(): everything = jax.tree.map(lambda part: lax.all_gather(part, axis), array)  215 us
    psum x1, blocking collectives, shards(): lax.psum((local_weight, local_bias, local_rates, local_skip), 'seq')  36.9 us
    select_n x16, other arithmetic, lap(): return jax.tree.map(lambda a, b: jnp.where(reached, a, b), new, before)  25.9 us
    all_gather x1, blocking collectives, carried_in(): everything = jax.tree.map(lambda part: lax.all_gather(part, axis), array)  19.1 us
    psum x1, blocking collectives, shards(): lax.psum(lax.psum((local_weight, local_bias, local_rates, local_skip), 's...  11.2 us
  transfers between devices with their start and end apart: 4, of which 2 were waited for; matrix products, arithmetic and copies ran while one was open for 17% of the time, Pallas kernels for 0%

profile of v1, /device:TPU:0, one launch (start us, length us, event | category | flops | bytes accessed | tf_op | source)
XLA Modules:
  0.0 461.6 jit_solution(10494560061629923237)
XLA Ops:
  8.0 4.9 %collective-permute-start = (bf16[1,3,2816]{2,1,0:T(4,128)(2,1)S(1)}, bf16[1,3,2816]{2,1,0:T(4,128)(2,1)S(1)}, u32[]{:S(2)}, u32[]{:S(2)}) collective-permute-start(bf16[1,3,2816]{2,1,0:T(4,128)(2,1)S(1)} %slice.105), channel_id=1, source_target_pairs={{0,1},{1,2},{2,3},{3,4},{4,5},{5,6},{6,7},{8,9},{9,10},{10,11},{11... | collective-permute-start | bytes 50696 | tf_op jit(solution)/shard_map/ppermute | solution.py:16
  14.9 1.7 broadcast_in_dim.65
  16.6 3.3 copy.237
  20.0 2.0 fusion.62
  22.7 1.4 copy.238
  24.2 4.4 multiply_convert_fusion.2
  29.7 1.7 convolution_add_fusion.1
  31.5 1.4 copy.231
  34.4 1.7 broadcast_in_dim.63
  36.1 3.2 copy.244
  39.3 3.6 copy.241
  42.9 19.1 %all-gather = f32[8,40,1]{1,2,0:T(1,128)S(1)} all-gather(f32[1,40,1]{1,2,0:T(1,128)S(1)} %get-tuple-element.432), channel_id=2, replica_groups=mesh['dp'=4,'seq'=8] {'seq'}, dimensions={0}, use_global_device_ids=true | all-gather | bytes 1440 | tf_op jit(solution)/shard_map/all_gather | solution.py:21
  63.3 5.4 %fusion.2 = f32[40,256,64]{1,2,0:T(8,128)} fusion(bf16[256,40,64]{0,2,1:T(8,128)(2,1)} %bitcast.195, f32[256,256]{0,1:T(8,128)S(1)} %copy.230, f32[40,256]{1,0:T(8,128)S(1)} %bitcast_add_fusion.3, pred[256,256]{0,1:T(8,128)(4,1)S(1)} %iota_compare_fusion.1), kind=kOutput, calls=%fused_computation.10 | convolution fusion | flops 348651520 | bytes 4300800 | tf_op jit(solution)/shard_map/vmap(hts,shp->thp)/dot_general | solution.py:92
  68.7 3.3 copy.242
  72.0 110.4 %all-gather.6.cloned.1.call-done = f32[320,64,128]{2,1,0:T(8,128)} async-done(((f32[40,64,128]{2,1,0:T(8,128)}), f32[320,64,128]{2,1,0:T(8,128)}) %all-gather.6.cloned.1.call-update) | async-done | bytes 10485776 | tf_op jit(solution)/shard_map/all_gather | solution.py:21
  182.3 13.3 %while.30 = (s32[]{:T(128)}, f32[1,40,64,128]{3,2,1,0:T(8,128)S(1)}, s32[]{:T(128)}, f32[8,1,40]{2,1,0:T(1,128)S(1)}, f32[8,1,40,64,128]{4,3,2,1,0:T(8,128)}, /*index=5*/s32[]{:T(128)}, s32[]{:T(128)}, s32[]{:T(128)}, s32[]{:T(128)}) while((s32[]{:T(128)}, f32[1,40,64,128]{3,2,1,0:T(8,128)S(1)}, s32[]{:T(128)}, ...), condition=%wide.region_3.4_spmd.clone, body=%wide.region_2.3_spmd.clone.sunk | while | flops 1310728 | bytes 3932815 | solution.py:34
  182.3 1.6 fusion.80
  184.0 1.6 fusion.80
  185.7 1.6 fusion.80
  187.4 1.6 fusion.80
  189.0 1.6 fusion.80
  190.7 1.6 fusion.80
  192.4 1.6 fusion.80
  194.0 1.6 fusion.80
  195.8 8.9 %convert_multiply_fusion.1 = (f32[1,256,2560]{2,1,0:T(8,128)}, f32[1,256,2560]{2,1,0:T(8,128)}, f32[1,256,2560]{2,1,0:T(8,128)}, f32[2560]{0:T(1024)}, bf16[2560,256]{0,1:T(8,128)(2,1)}) fusion(f32[256,2560]{1,0:T(8,128)} %copy.242, f32[256,2560]{1,0:T(8,128)} %copy.241, bf16[1,256,2816]{2,1,0:T(8,128)(2,1)} %copy-done.2, ...), kind=kOutput, calls=%fused_computation.17 | convolution fusion | flops 175633920 | bytes 20402176 | tf_op jit(solution)/shard_map/vmap()/dot_general | solution.py:88
  204.8 1.6 copy.247
  206.4 2.4 convolution_add_fusion
  210.0 2.5 slice.138
  212.4 2.5 copy.243
  214.9 7.5 %multiply_reduce_fusion.1 = (f32[40,256]{1,0:T(8,128)S(1)}, f32[40,256]{1,0:T(8,128)S(1)}, bf16[256,256]{0,1:T(8,128)(2,1)S(1)}) fusion(f32[256,256]{0,1:T(8,128)} %bitcast.198, f32[40,256]{1,0:T(8,128)} %copy-done.27, pred[256,256]{0,1:T(8,128)(4,1)} %iota_compare_fusion, bf16[256,40,64]{0,2,1:T(8,128)(2,1)} %bitcast.197, bf16[256,40,64]{0,2,1:T(8,128)(2,1)} %bitcast.196), kind=kOutput, calls=%fused_computation.9 | convolution fusion | flops 356429824 | bytes 3203072 | tf_op jit(solution)/shard_map/vmap(thp,shp->hts)/dot_general | solution.py:81
  223.7 1.4 sub.92
  225.1 1.4 copy.252
  226.5 1.9 reduce-window.30
  228.4 1.4 copy.253
  229.8 1.5 slice_reduce_fusion.2
  232.6 1.4 copy.254
  234.0 3.3 copy.265
  237.3 2.6 reduce_sum.150
  239.9 1.4 reduce_sum.159
  242.1 3.3 copy.260
  245.4 2.6 reduce_sum.147
  248.0 1.5 copy.261
  249.6 2.6 fusion.24
  253.2 104.4 %all-gather.8.cloned.1.call-done = f32[320,64,128]{2,1,0:T(8,128)} async-done(((f32[40,64,128]{2,1,0:T(8,128)}), f32[320,64,128]{2,1,0:T(8,128)}) %all-gather.8.cloned.1.call-update) | async-done | bytes 10485776 | tf_op jit(solution)/shard_map/all_gather | solution.py:21
  357.6 18.2 %while.31 = (s32[]{:T(128)}, f32[1,40,64,128]{3,2,1,0:T(8,128)S(1)}, s32[]{:T(128)}, f32[8,1,40]{2,1,0:T(1,128)}, f32[8,1,40,64,128]{4,3,2,1,0:T(8,128)}, /*index=5*/s32[]{:T(128)}, s32[]{:T(128)}) while((s32[]{:T(128)}, f32[1,40,64,128]{3,2,1,0:T(8,128)S(1)}, s32[]{:T(128)}, f32[8,1,40]{2,1,0:T(1,128)}, ...), condition=%wide.region_6.7_spmd.clone, body=%wide.region_5.6_spmd.clone.sunk | while | flops 1310724 | bytes 3932753 | solution.py:34
  358.2 1.6 fusion.81
  360.5 1.6 fusion.81
  362.8 1.6 fusion.81
  365.0 1.6 fusion.81
  367.3 1.6 fusion.81
  369.6 1.6 fusion.81
  371.9 1.6 fusion.81
  374.2 1.6 fusion.81
  377.2 2.6 fusion.26
  380.9 4.7 %fusion.13 = (f32[2816]{0:T(1024)S(1)}, f32[2816]{0:T(1024)S(1)}, f32[2816]{0:T(1024)S(1)}, f32[2816]{0:T(1024)S(1)}, f32[2816]{0:T(1024)S(1)}, /*index=5*/f32[1,256,2816]{2,1,0:T(8,128)S(1)}) fusion(bf16[1,256,2816]{2,1,0:T(8,128)(2,1)S(1)} %copy-done.4, bf16[1,3,2816]{2,1,0:T(4,128)(2,1)S(1)} %copy-done.20, f32[2816]{0:T(1024)S(1)} %copy-done.13, ...), kind=kLoop, calls=%fused_computation.37 | loop fusion | flops 34588928 | bytes 7338496 | tf_op jit(solution)/shard_map/reduce_sum | solution.py:209
  385.6 2.8 multiply_add_fusion
  388.4 2.9 convert_multiply_fusion.4
  391.3 3.2 copy.255
  394.5 2.1 reduce_sum.145
  398.8 1.3 collective-permute-start.1
  400.1 2.0 slice.261
  404.5 36.9 %all-reduce.2 = (f32[4,2816]{1,0:T(4,128)S(1)}, f32[2816]{0:T(1024)S(1)}, f32[40]{0:T(128)S(1)}, f32[40]{0:T(128)S(1)}) all-reduce(f32[4,2816]{1,0:T(4,128)S(1)} %pad_maximum_fusion.2, f32[2816]{0:T(1024)S(1)} %get-tuple-element.383, f32[40]{0:T(128)S(1)} %neg.16, f32[40]{0:T(128)S(1)} %reduce_sum.160), channel_id=1, replica_groups=mesh['dp'=4,'seq'=8] {'seq'}, use_global_device_ids=true, to_apply=%region_23.24 | all-reduce | flops 14160 | bytes 113280 | tf_op jit(solution)/shard_map/psum | solution.py:219
  441.4 11.2 %all-reduce.3 = (f32[4,2816]{1,0:T(4,128)}, f32[2816]{0:T(1024)}, f32[40]{0:T(128)}, f32[40]{0:T(128)}) all-reduce(f32[4,2816]{1,0:T(4,128)S(1)} %get-tuple-element.409, f32[2816]{0:T(1024)S(1)} %get-tuple-element.410, f32[40]{0:T(128)S(1)} %get-tuple-element.411, f32[40]{0:T(128)S(1)} %get-tuple-element.412), channel_id=1, replica_groups=mesh['dp'=4,'seq'=8] {'dp'}, use_global_device_ids=true, to_apply=%region_24.25 | all-reduce | flops 14160 | bytes 113280 | tf_op jit(solution)/shard_map/psum | solution.py:218
  453.6 1.2 pad_maximum_fusion.1
  (163 shorter events, 25.8 us)
Async XLA Ops:
  7.2 175.2 %all-gather.6.cloned.1.call-start = ((), (), s32[]{:S(2)}) async-start(), calls=%async_computation | async-start | bytes 11796480 | tf_op jit(solution)/shard_map/all_gather | solution.py:21
  8.0 16.1 %collective-permute-start = (bf16[1,3,2816]{2,1,0:T(4,128)(2,1)S(1)}, bf16[1,3,2816]{2,1,0:T(4,128)(2,1)S(1)}, u32[]{:S(2)}, u32[]{:S(2)}) collective-permute-start(bf16[1,3,2816]{2,1,0:T(4,128)(2,1)S(1)} %slice.105), channel_id=1, source_target_pairs={{0,1},{1,2},{2,3},{3,4},{4,5},{5,6},{6,7},{8,9},{9,10},{10,11},{11... | collective-permute-start | bytes 50696 | tf_op jit(solution)/shard_map/ppermute | solution.py:16
  16.6 3.4 copy-start
  20.0 2.0 copy-start.26
  22.0 2.1 copy-start.22
  22.7 5.9 %copy-start.8 = (f32[2816]{0:T(1024)}, f32[2816]{0:T(1024)S(1)}, u32[]{:S(2)}) copy-start(f32[2816]{0:T(1024)S(1)} %get-tuple-element.386) | copy-start | bytes 33796
  22.7 5.9 %copy-start.10 = (f32[2816]{0:T(1024)}, f32[2816]{0:T(1024)S(1)}, u32[]{:S(2)}) copy-start(f32[2816]{0:T(1024)S(1)} %get-tuple-element.388) | copy-start | bytes 33796
  22.7 5.9 %copy-start.12 = (f32[2816]{0:T(1024)}, f32[2816]{0:T(1024)S(1)}, u32[]{:S(2)}) copy-start(f32[2816]{0:T(1024)S(1)} %get-tuple-element.387) | copy-start | bytes 33796
  24.1 5.6 %copy-start.5 = (bf16[2560,256]{1,0:T(8,128)(2,1)S(1)}, bf16[2560,256]{1,0:T(8,128)(2,1)}, u32[]{:S(2)}) copy-start(bf16[2560,256]{1,0:T(8,128)(2,1)} %copy.238) | copy-start | bytes 3932164
  24.2 7.2 %copy-start.19 = (bf16[1,3,2816]{2,1,0:T(4,128)(2,1)}, bf16[1,3,2816]{2,1,0:T(4,128)(2,1)S(1)}, u32[]{:S(2)}) copy-start(bf16[1,3,2816]{2,1,0:T(4,128)(2,1)S(1)} %collective-permute-done) | copy-start | bytes 50692
  28.6 1.1 copy-start.2
  31.4 1.5 copy-start.33
  31.4 326.2 %all-gather.8.cloned.1.call-start = ((), (), s32[]{:S(2)}) async-start(), calls=%async_computation.1 | async-start | bytes 11796480 | tf_op jit(solution)/shard_map/all_gather | solution.py:21
  33.8 0.5 copy-start.29
  62.0 6.7 %copy-start.27 = (f32[40,256]{1,0:T(8,128)}, f32[40,256]{1,0:T(8,128)S(1)}, u32[]{:S(2)}) copy-start(f32[40,256]{1,0:T(8,128)S(1)} %bitcast_add_fusion.3) | copy-start | bytes 122884
  63.1 5.6 %copy-start.6 = (f32[256,256]{1,0:T(8,128)}, f32[256,256]{1,0:T(8,128)S(1)}, u32[]{:S(2)}) copy-start(f32[256,256]{1,0:T(8,128)S(1)} %fusion.35) | copy-start | bytes 786436
  182.3 13.4 %copy-start.24 = (f32[2560]{0:T(1024)S(1)}, f32[2560]{0:T(1024)}, u32[]{:S(2)}) copy-start(f32[2560]{0:T(1024)} %mul.301) | copy-start | bytes 30724
  195.7 9.1 %copy-start.28 = (f32[8,1,40]{2,1,0:T(1,128)}, f32[8,1,40]{2,1,0:T(1,128)S(1)}, u32[]{:S(2)}) copy-start(f32[8,1,40]{2,1,0:T(1,128)S(1)} %get-tuple-element.555) | copy-start | bytes 3844
  206.3 2.4 copy-start.31
  222.5 0.6 copy-start.16
  375.8 1.3 copy-start.1
  376.3 4.6 copy-start.3
  376.3 4.6 copy-start.4
  376.3 4.6 copy-start.9
  376.3 4.6 copy-start.11
  376.3 4.6 copy-start.13
  376.3 4.6 copy-start.20
  376.3 4.6 copy-start.23
  394.5 2.2 copy-start.7
  394.5 2.2 copy-start.30
  394.5 4.2 copy-start.25
  396.6 6.3 %copy-start.21 = (f32[40,2]{1,0:T(8,128)S(1)}, f32[40,2]{1,0:T(8,128)}, u32[]{:S(2)}) copy-start(f32[40,2]{1,0:T(8,128)} %copy.254) | copy-start | bytes 964
  396.7 6.4 %copy-start.14 = (f32[1,40,256]{2,1,0:T(8,128)S(1)}, f32[1,40,256]{2,1,0:T(8,128)}, u32[]{:S(2)}) copy-start(f32[1,40,256]{2,1,0:T(8,128)} %param.14) | copy-start | bytes 122884
  396.7 6.4 %copy-start.15 = (f32[1,40,2,128]{3,2,0,1:T(2,128)S(1)}, f32[1,40,2,128]{3,2,0,1:T(2,128)}, u32[]{:S(2)}) copy-start(f32[1,40,2,128]{3,2,0,1:T(2,128)} %copy.253) | copy-start | bytes 122884
  396.7 6.4 %copy-start.17 = (f32[40,256]{1,0:T(8,128)S(1)}, f32[40,256]{1,0:T(8,128)}, u32[]{:S(2)}) copy-start(f32[40,256]{1,0:T(8,128)} %copy-done.16) | copy-start | bytes 122884
  396.7 6.4 %copy-start.18 = (f32[256,40]{0,1:T(8,128)S(1)}, f32[256,40]{0,1:T(8,128)}, u32[]{:S(2)}) copy-start(f32[256,40]{0,1:T(8,128)} %reduce_sum.150) | copy-start | bytes 122884
  396.8 6.9 %copy-start.32 = (f32[40]{0:T(128)S(1)}, f32[40]{0:T(128)}, u32[]{:S(2)}) copy-start(f32[40]{0:T(128)} %neg.15) | copy-start | bytes 484
  398.8 53.9 %collective-permute-start.1 = (f32[1,3,2816]{2,1,0:T(4,128)S(1)}, f32[1,3,2816]{2,1,0:T(4,128)S(1)}, u32[]{:S(2)}, u32[]{:S(2)}) collective-permute-start(f32[1,3,2816]{2,1,0:T(4,128)S(1)} %fusion.46), channel_id=1, source_target_pairs={{1,0},{2,1},{3,2},{4,3},{5,4},{6,5},{7,6},{9,8},{10,9},{11,10},{12... | collective-permute-start | bytes 101384 | tf_op jit(solution)/shard_map/ppermute | solution.py:16
Sparse Core Ops, SparseCore 0:
  31.6 150.7 all-gather.5
  208.9 148.6 all-gather.7
